TPU v7x, 32 devices: a whole 2x2x4 slice. The times are simulated.
32 devices in a mesh: groups: 2 (over x), seq: 8 (over z, y), chan: 2 (over core).
Axes of the slice: x: 2, y: 2, z: 4, core: 2. Of those that a mesh axis runs over, the one named last changes fastest.
Arguments:
- stream: bfloat16 [4096, 2048], P(('groups', 'seq'), 'chan'), parts along dimension 0, may hold values from -6 to 6
- nucleotide_token_ids: int32 [4096], P(('groups', 'seq')), parts along dimension 0, may hold values from 4 to 11, as said below
- genome_length: int32 [2], P('groups'), parts along dimension 0, may hold values from 1024 to 2048
- embedding: bfloat16 [16, 2048], replicated, may hold values from -6 to 6
- attention_in: bfloat16 [2048, 3, 1024], P(None, None, 'chan'), may hold values from -0.125 to 0.125
- scan_input: bfloat16 [2048, 1024], P(None, 'chan'), may hold values from -0.125 to 0.125
- state_maps: bfloat16 [2048, 256], P(None, 'chan'), may hold values from -0.125 to 0.125
- step_weight: bfloat16 [2048, 8], P(None, 'chan'), may hold values from -0.125 to 0.125
- step_bias: float32 [8], P('chan'), may hold values from -1 to 1
- head_decay_speed: float32 [8], P('chan'), as said below
- attention_gain: float32 [1024], P('chan'), may hold values from 0.25 to 1.75
- scan_gain: float32 [1024], P('chan'), may hold values from 0.25 to 1.75
- out_weight: bfloat16 [1024, 2048], P('chan'), may hold values from -0.1875 to 0.1875
Outputs:
- block_out: bfloat16 [4096, 2048], P(('groups', 'seq'), 'chan'), parts along dimension 0
There are 2 independent parts, one for each index of `groups`. A program takes and returns all parts, laid end to end along the dimension named above; an argument that names none is the same for every part. Nothing has to cross between parts.
Inputs may be any that keep to these rules, and one draw needn't show every extreme that they name: `nucleotide_token_ids`: positions below genome_length hold bases 7 to 10, except exactly three positions that hold 11, one in each third of the valid range; positions at or above genome_length hold 4. `head_decay_speed`: every entry lies between 1 / 20480 and 8 / 256.
All inputs are finite; a program needn't handle non-finite values.
Results may differ from a plain program's by a relative error of at most 0.0058.
Values may be sent and summed in bfloat16 or wider, within the bound.
A program may use at most 128 MiB of HBM per device.

v0:
```python
import math
import jax
import jax.numpy as jnp
from jax import lax
from jax.sharding import PartitionSpec as P

HEAD_DIM = 128
STATE = 64
epsilon_norm = 1e-06
spike_logarithm = math.log(0.7)
unclear_nucleotide = 11


def passed_along(block, axis, distance):
    devices = range(lax.axis_size(axis))
    route = [((i - distance) % len(devices), i) for i in devices]
    return lax.ppermute(block, axis, route)


def normalize(values):
    return values * lax.rsqrt(jnp.mean(values * values, axis=-1, keepdims=True) + epsilon_norm)


def compose(earlier_part, later_part):
    return (
        earlier_part[0] * later_part[0],
        later_part[0][:, None, None] * earlier_part[1] + later_part[1],
    )


def key_block(query_tile_rows, key_fragment, value_piece, key_position, valid_limit, score_scale):
    scores = (
        jnp.einsum(
            "epq,fpq->pef", query_tile_rows, key_fragment, preferred_element_type=jnp.float32
        )
        * score_scale
    )
    weights = jnp.where((key_position < valid_limit)[None, None, :], jnp.exp(scores), 0.0)
    totals = jnp.sum(weights, axis=-1).T
    numerator = jnp.einsum(
        "gfa,agn->fgn",
        weights.astype(jnp.bfloat16),
        value_piece,
        preferred_element_type=jnp.float32,
    )
    return (numerator, totals)


def local(
    stream,
    nucleotide_token_ids,
    genome_length,
    embedding,
    attention_in,
    scan_input,
    state_maps,
    step_weight,
    step_bias,
    head_decay_speed,
    attention_gain,
    scan_gain,
    out_weight,
):
    row_count = stream.shape[0]
    model_width = embedding.shape[1]
    head_count = step_weight.shape[1]
    score_scale = 2.0 / math.sqrt(HEAD_DIM)
    valid_limit = genome_length[0]
    position = lax.axis_index("seq") * row_count + jnp.arange(row_count, dtype=jnp.int32)
    key_valid = position < valid_limit
    gathered = lax.all_gather(stream, "chan", axis=1, tiled=True)
    onehot = (
        nucleotide_token_ids[:, None] == jnp.arange(embedding.shape[0], dtype=jnp.int32)[None, :]
    ).astype(jnp.bfloat16)
    hidden = (
        gathered.astype(jnp.float32)
        + jnp.dot(onehot, embedding, preferred_element_type=jnp.float32)
    ).astype(jnp.bfloat16)
    projected = jnp.dot(
        hidden,
        attention_in.reshape(model_width, 3 * head_count * HEAD_DIM),
        preferred_element_type=jnp.float32,
    ).reshape(row_count, 3, head_count, HEAD_DIM)
    queries = normalize(projected[:, 0]).astype(jnp.bfloat16)
    keyset = normalize(projected[:, 1]).astype(jnp.bfloat16)
    valueset = projected[:, 2].astype(jnp.bfloat16)
    empty_numer = jnp.zeros((row_count, head_count, HEAD_DIM), jnp.float32)
    empty_total = jnp.zeros((row_count, head_count), jnp.float32)
    carry_pair = (empty_numer, empty_total)
    key_fragment = lax.all_gather(keyset, "seq", axis=0, tiled=True)
    value_piece = lax.all_gather(valueset, "seq", axis=0, tiled=True)
    piece_rows = key_fragment.shape[0]
    block_count = piece_rows // 512

    def absorb_block(running, element):
        key_block_rows, value_block_rows, first_row = element
        numer_part, total_part = key_block(
            queries,
            key_block_rows,
            value_block_rows,
            first_row + jnp.arange(512, dtype=jnp.int32),
            valid_limit,
            score_scale,
        )
        return ((running[0] + numer_part, running[1] + total_part), None)

    first_rows = 512 * jnp.arange(block_count, dtype=jnp.int32)
    carry_pair, _ = lax.scan(
        absorb_block,
        carry_pair,
        (
            key_fragment.reshape(block_count, 512, head_count, HEAD_DIM),
            value_piece.reshape(block_count, 512, head_count, HEAD_DIM),
            first_rows,
        ),
    )
    numerator, totals = carry_pair
    attended = normalize(numerator / totals[:, :, None])
    inputs = (
        jax.nn.silu(jnp.dot(hidden, scan_input, preferred_element_type=jnp.float32))
        .astype(jnp.bfloat16)
        .reshape(row_count, head_count, HEAD_DIM)
    )
    state_rows = jax.nn.silu(
        jnp.dot(hidden, state_maps, preferred_element_type=jnp.float32)
    ).astype(jnp.bfloat16)
    input_map = state_rows[:, :STATE]
    output_map = state_rows[:, STATE:]
    step_list = jax.nn.softplus(
        jnp.dot(hidden, step_weight, preferred_element_type=jnp.float32) + step_bias[None, :]
    )
    usable_rows = key_valid.astype(jnp.float32)[:, None]
    spike_events = jnp.where(nucleotide_token_ids == unclear_nucleotide, spike_logarithm, 0.0)[
        :, None
    ]
    logarithm_decay = usable_rows * (-head_decay_speed[None, :] * step_list + spike_events)
    used_steps = usable_rows * step_list
    forward = jnp.cumsum(logarithm_decay, axis=0)
    backward = jnp.flip(jnp.cumsum(jnp.flip(logarithm_decay, 0), axis=0), 0)
    inputs_wide = inputs.astype(jnp.float32)
    scaled_forward = (
        (jnp.exp(forward[-1:] - forward) * used_steps)[:, :, None] * inputs_wide
    ).astype(jnp.bfloat16)
    scaled_backward = (
        (jnp.exp(backward[:1] - backward) * used_steps)[:, :, None] * inputs_wide
    ).astype(jnp.bfloat16)
    own_forward = (
        jnp.exp(forward[-1]),
        jnp.einsum("the,ts->hes", scaled_forward, input_map, preferred_element_type=jnp.float32),
    )
    own_backward = (
        jnp.exp(backward[0]),
        jnp.einsum("the,ts->hes", scaled_backward, input_map, preferred_element_type=jnp.float32),
    )
    section_count = lax.axis_size("seq").bit_length() - 1
    distances = [1] + [1 << section for section in range(section_count)]
    window_forward = own_forward
    window_backward = own_backward
    for section_index, distance in enumerate(distances):
        received_up = passed_along((window_forward[0], window_forward[1]), "seq", distance)
        received_down = passed_along((window_backward[0], window_backward[1]), "seq", -distance)
        if section_index == 0:
            window_forward = received_up
            window_backward = received_down
        else:
            window_forward = compose(received_up, window_forward)
            window_backward = compose(received_down, window_backward)
    enter_forward = window_forward[1] / (1.0 - window_forward[0])[:, None, None]
    enter_backward = window_backward[1] / (1.0 - window_backward[0])[:, None, None]
    pairing = jnp.dot(output_map, input_map.T, preferred_element_type=jnp.float32)
    block_rows = jnp.arange(row_count)
    causal_mask = block_rows[:, None] >= block_rows[None, :]
    read_wide = output_map.astype(jnp.float32)

    def strand(cumulative, allowed, entering):
        across = cumulative.T
        exponent = across[:, :, None] - across[:, None, :]
        mixing = (
            pairing[None]
            * jnp.exp(jnp.where(allowed[None], exponent, -jnp.inf))
            * used_steps.T[:, None, :]
        ).astype(jnp.bfloat16)
        local_part = jnp.einsum("htu,uhe->the", mixing, inputs, preferred_element_type=jnp.float32)
        carried = jnp.exp(cumulative)[:, :, None] * jnp.einsum(
            "ts,hes->the", read_wide, entering, precision=lax.Precision.HIGHEST
        )
        return local_part + carried

    scanned = normalize(
        strand(forward, causal_mask, enter_forward)
        + strand(backward, causal_mask.T, enter_backward)
    )
    combined = (
        (
            attention_gain.reshape(head_count, HEAD_DIM) * attended
            + scan_gain.reshape(head_count, HEAD_DIM) * scanned
        )
        .astype(jnp.bfloat16)
        .reshape(row_count, head_count * HEAD_DIM)
    )
    partial_out = jnp.dot(combined, out_weight, preferred_element_type=jnp.float32)
    summed = lax.psum_scatter(partial_out, "chan", scatter_dimension=1, tiled=True)
    return (stream.astype(jnp.float32) + summed).astype(jnp.bfloat16)


def solution(mesh):
    placed = (
        P(("groups", "seq"), "chan"),
        P(("groups", "seq")),
        P("groups"),
        P(),
        P(None, None, "chan"),
        P(None, "chan"),
        P(None, "chan"),
        P(None, "chan"),
        P("chan"),
        P("chan"),
        P("chan"),
        P("chan"),
        P("chan", None),
    )
    return jax.shard_map(
        local, mesh=mesh, in_specs=placed, out_specs=P(("groups", "seq"), "chan"), check_vma=False
    )
```

profile of v0, /device:TPU:0, one launch (start us, length us, event | category | flops | bytes accessed | tf_op | source)
XLA Modules:
  0.0 197.7 jit_solution(5060600774243856370)
XLA Ops:
  7.3 8.9 %copy.26 = bf16[2048,3,512]{0,2,1:T(8,128)(2,1)} copy(bf16[2048,3,512]{2,0,1:T(8,128)(2,1)} %param.19) | data formatting | bytes 12582912 | tf_op args[4]
  16.2 4.4 %all-gather.5.cloned.1.call-done = bf16[256,2048]{1,0:T(8,128)(2,1)} async-done(((bf16[256,1024]{1,0:T(8,128)(2,1)}), bf16[256,2048]{1,0:T(8,128)(2,1)}) %all-gather.5.cloned.1.call-update) | async-done | bytes 1048592 | tf_op jit(solution)/shard_map/all_gather | solution.py:71
  22.4 5.0 %fusion.17 = f32[256,3,4,128]{0,3,2,1:T(8,128)S(1)} fusion(bf16[3,4,128,2048]{3,2,1,0:T(8,128)(2,1)} %bitcast.158, bf16[256,2048]{1,0:T(8,128)(2,1)S(1)} %fusion.13), kind=kOutput, calls=%fused_computation.29 | convolution fusion | flops 1610612736 | bytes 8912896 | tf_op jit(solution)/shard_map/dot_general | solution.py:79
  41.5 2.7 %fusion.43 = bf16[32,4,8,128]{3,2,1,0:T(8,128)(2,1)S(1)} fusion(bf16[256,2048]{1,0:T(8,128)(2,1)} %copy-done.3, bf16[2048,512]{1,0:T(8,128)(2,1)} %param.20), kind=kOutput, calls=%fused_computation.72 | convolution fusion | flops 537526272 | bytes 3407872 | tf_op jit(solution)/shard_map/dot_general | solution.py:120
  49.5 3.2 %collective-permute-start.8 = (f32[4]{0:T(128)}, f32[4]{0:T(128)}, u32[]{:S(2)}, u32[]{:S(2)}) collective-permute-start(f32[4]{0:T(128)} %exp.54), channel_id=1, source_target_pairs={{2,0},{4,2},{6,4},{8,6},{10,8},{12,10},{14,12},{0,14},{3,1},{5,3},... | collective-permute-start | bytes 56 | tf_op jit(solution)/shard_map/ppermute | solution.py:17
  58.4 3.0 %collective-permute-start.9 = (f32[4]{0:T(128)}, f32[4]{0:T(128)S(1)}, u32[]{:S(2)}, u32[]{:S(2)}) collective-permute-start(f32[4]{0:T(128)} %collective-permute-done.8), channel_id=1, source_target_pairs={{2,0},{4,2},{6,4},{8,6},{10,8},{12,10},{14,12},{0,14},{3,1},{5,3},... | collective-permute-start | bytes 56 | tf_op jit(solution)/shard_map/ppermute | solution.py:17
  64.4 3.8 %collective-permute-start.10 = (f32[4]{0:T(128)S(1)}, f32[4]{0:T(128)S(1)}, u32[]{:S(2)}, u32[]{:S(2)}) collective-permute-start(f32[4]{0:T(128)S(1)} %mul.298), channel_id=1, source_target_pairs={{4,0},{6,2},{8,4},{10,6},{12,8},{14,10},{0,12},{2,14},{5,1},{7,3},... | collective-permute-start | bytes 56 | tf_op jit(solution)/shard_map/ppermute | solution.py:17
  69.5 2.5 %collective-permute-start.15 = (f32[4]{0:T(128)S(1)}, f32[4]{0:T(128)S(1)}, u32[]{:S(2)}, u32[]{:S(2)}) collective-permute-start(f32[4]{0:T(128)S(1)} %mul.299), channel_id=1, source_target_pairs={{8,0},{10,2},{12,4},{14,6},{0,8},{2,10},{4,12},{6,14},{9,1},{11,3}... | collective-permute-start | bytes 56 | tf_op jit(solution)/shard_map/ppermute | solution.py:17
  75.7 3.8 %collective-permute-done.12 = f32[4,128,64]{1,2,0:T(8,128)S(1)} collective-permute-done((f32[4,128,64]{1,2,0:T(8,128)S(1)}, f32[4,128,64]{1,2,0:T(8,128)S(1)}, u32[]{:S(2)}, u32[]{:S(2)}) %collective-permute-start.12) | collective-permute-done | bytes 131104 | tf_op jit(solution)/shard_map/ppermute | solution.py:17
  82.1 3.3 %collective-permute-done.4 = f32[4,128,64]{1,2,0:T(8,128)S(1)} collective-permute-done((f32[4,128,64]{1,2,0:T(8,128)S(1)}, f32[4,128,64]{1,2,0:T(8,128)S(1)}, u32[]{:S(2)}, u32[]{:S(2)}) %collective-permute-start.4) | collective-permute-done | bytes 131104 | tf_op jit(solution)/shard_map/ppermute | solution.py:17
  86.7 7.5 %collective-permute-start.14 = (f32[4,128,64]{1,2,0:T(8,128)S(1)}, f32[4,128,64]{1,2,0:T(8,128)S(1)}, u32[]{:S(2)}, u32[]{:S(2)}) collective-permute-start(f32[4,128,64]{1,2,0:T(8,128)S(1)} %multiply_add_fusion), channel_id=1, source_target_pairs={{8,0},{10,2},{12,4},{14,6},{0,8},{2,10},{4,12},{6,14},{9,1},{11,3}... | collective-permute-start | bytes 393224 | tf_op jit(solution)/shard_map/ppermute | solution.py:17
  94.2 3.7 %collective-permute-done.5 = f32[4,128,64]{1,2,0:T(8,128)S(1)} collective-permute-done((f32[4,128,64]{1,2,0:T(8,128)S(1)}, f32[4,128,64]{1,2,0:T(8,128)S(1)}, u32[]{:S(2)}, u32[]{:S(2)}) %collective-permute-start.5) | collective-permute-done | bytes 131104 | tf_op jit(solution)/shard_map/ppermute | solution.py:17
  102.0 6.3 %collective-permute-done.6 = f32[4,128,64]{1,2,0:T(8,128)S(1)} collective-permute-done((f32[4,128,64]{1,2,0:T(8,128)S(1)}, f32[4,128,64]{1,2,0:T(8,128)S(1)}, u32[]{:S(2)}, u32[]{:S(2)}) %collective-permute-start.6) | collective-permute-done | bytes 131104 | tf_op jit(solution)/shard_map/ppermute | solution.py:17
  108.8 4.5 %reshape.152 = bf16[4,512,4,128]{1,0,3,2:T(4,128)(2,1)} reshape(bf16[2048,4,128]{0,2,1:T(8,128)(2,1)} %all-gather.7.cloned.1.call-done) | data formatting | bytes 4194304 | tf_op jit(solution)/shard_map/reshape | solution.py:112
  113.3 4.5 %copy.28 = bf16[4,512,4,128]{3,1,2,0:T(8,128)(2,1)} copy(bf16[4,512,4,128]{1,0,3,2:T(4,128)(2,1)} %reshape.152) | data formatting | bytes 4194304
  117.8 24.4 %all-gather.9.cloned.1.call-done = bf16[2048,1,4,128]{0,3,2,1:T(8,128)(2,1)} async-done(((bf16[256,1,4,128]{0,3,2,1:T(8,128)(2,1)}), bf16[2048,1,4,128]{0,3,2,1:T(8,128)(2,1)}) %all-gather.9.cloned.1.call-update) | async-done | bytes 2097168 | tf_op jit(solution)/shard_map/all_gather | solution.py:91
  142.3 4.5 %reshape.151 = bf16[4,512,4,128]{1,0,3,2:T(4,128)(2,1)} reshape(bf16[2048,1,4,128]{0,3,2,1:T(8,128)(2,1)} %all-gather.9.cloned.1.call-done) | data formatting | bytes 4194304 | tf_op jit(solution)/shard_map/reshape | solution.py:113
  146.8 3.4 %copy.27 = bf16[4,512,4,128]{1,3,2,0:T(8,128)(2,1)} copy(bf16[4,512,4,128]{1,0,3,2:T(4,128)(2,1)} %reshape.151) | data formatting | bytes 4194304
  150.1 28.5 %while.13 = (s32[]{:T(128)}, f32[256,4,128]{0,2,1:T(8,128)S(1)}, f32[256,4]{0,1:T(4,128)S(1)}, bf16[4,512,4,128]{1,3,2,0:T(8,128)(2,1)}, s32[4]{0:T(128)S(1)}, /...) while((s32[]{:T(128)}, f32[256,4,128]{0,2,1:T(8,128)S(1)}, ...), condition=%wide.region_4.5_spmd.clone, body=%wide.region_2.4_spmd.clone.sunk | while | flops 271845376 | bytes 6572676 | solution.py:108
  152.0 2.9 %bitcast_reduce_fusion.2 = (f32[4,256]{1,0:T(4,128)S(1)}, f32[4,512,256]{2,1,0:T(8,128)}) fusion(pred[512]{0:T(512)(128)(4,1)S(1)} %add_compare_fusion.2, bf16[256,4,128]{2,0,1:T(8,128)(2,1)S(1)} %get-tuple-element.209, bf16[4,512,4,128]{3,1,2,0:T(8,128)(2,1)} %get-tuple-element.208, s32[]{:T(128)} %get-tuple-element.192), kind=kOutput, calls=%fused_computation.clone.1 | convolution fusion | flops 135789568 | bytes 2888704 | tf_op jit(solution)/shard_map/while/body/eval_jaxpr/epq,fpq->pef/dot_general | solution.py:33
  159.2 2.9 %bitcast_reduce_fusion.2 = (f32[4,256]{1,0:T(4,128)S(1)}, f32[4,512,256]{2,1,0:T(8,128)}) fusion(pred[512]{0:T(512)(128)(4,1)S(1)} %add_compare_fusion.2, bf16[256,4,128]{2,0,1:T(8,128)(2,1)S(1)} %get-tuple-element.209, bf16[4,512,4,128]{3,1,2,0:T(8,128)(2,1)} %get-tuple-element.208, s32[]{:T(128)} %get-tuple-element.192), kind=kOutput, calls=%fused_computation.clone.1 | convolution fusion | flops 135789568 | bytes 2888704 | tf_op jit(solution)/shard_map/while/body/eval_jaxpr/epq,fpq->pef/dot_general | solution.py:33
  166.3 2.9 %bitcast_reduce_fusion.2 = (f32[4,256]{1,0:T(4,128)S(1)}, f32[4,512,256]{2,1,0:T(8,128)}) fusion(pred[512]{0:T(512)(128)(4,1)S(1)} %add_compare_fusion.2, bf16[256,4,128]{2,0,1:T(8,128)(2,1)S(1)} %get-tuple-element.209, bf16[4,512,4,128]{3,1,2,0:T(8,128)(2,1)} %get-tuple-element.208, s32[]{:T(128)} %get-tuple-element.192), kind=kOutput, calls=%fused_computation.clone.1 | convolution fusion | flops 135789568 | bytes 2888704 | tf_op jit(solution)/shard_map/while/body/eval_jaxpr/epq,fpq->pef/dot_general | solution.py:33
  173.4 2.9 %bitcast_reduce_fusion.2 = (f32[4,256]{1,0:T(4,128)S(1)}, f32[4,512,256]{2,1,0:T(8,128)}) fusion(pred[512]{0:T(512)(128)(4,1)S(1)} %add_compare_fusion.2, bf16[256,4,128]{2,0,1:T(8,128)(2,1)S(1)} %get-tuple-element.209, bf16[4,512,4,128]{3,1,2,0:T(8,128)(2,1)} %get-tuple-element.208, s32[]{:T(128)} %get-tuple-element.192), kind=kOutput, calls=%fused_computation.clone.1 | convolution fusion | flops 135789568 | bytes 2888704 | tf_op jit(solution)/shard_map/while/body/eval_jaxpr/epq,fpq->pef/dot_general | solution.py:33
  181.1 7.9 %reduce-scatter.2.cloned.1.call-done = f32[256,1024]{1,0:T(8,128)} async-done(((f32[256,2048]{1,0:T(8,128)}), f32[256,1024]{1,0:T(8,128)}) %reduce-scatter.2.cloned.1.call-update) | async-done | bytes 1048592 | tf_op jit(solution)/shard_map/reduce_scatter | solution.py:202
  (145 shorter events, 64.4 us)
Async XLA Ops:
  6.5 172.5 %copy-start = (bf16[512,2048]{1,0:T(8,128)(2,1)S(1)}, bf16[512,2048]{1,0:T(8,128)(2,1)}, u32[]{:S(2)}) copy-start(bf16[512,2048]{1,0:T(8,128)(2,1)} %param.27) | copy-start | bytes 6291460
  6.5 14.1 %all-gather.5.cloned.1.call-start = ((), (), s32[]{:S(2)}) async-start(), calls=%async_computation.1 | async-start | bytes 1572864 | tf_op jit(solution)/shard_map/all_gather | solution.py:71
  7.3 13.4 %copy-start.4 = (bf16[16,2048]{1,0:T(8,128)(2,1)S(1)}, bf16[16,2048]{1,0:T(8,128)(2,1)}, u32[]{:S(2)}) copy-start(bf16[16,2048]{1,0:T(8,128)(2,1)} %param.18) | copy-start | bytes 196612
  7.3 101.5 %all-gather.7.cloned.1.call-start = ((), (), s32[]{:S(2)}) async-start(), calls=%async_computation.2 | async-start | bytes 2359296 | tf_op jit(solution)/shard_map/all_gather | solution.py:90
  29.4 112.8 %all-gather.9.cloned.1.call-start = ((), (), s32[]{:S(2)}) async-start(), calls=%async_computation.4 | async-start | bytes 2359296 | tf_op jit(solution)/shard_map/all_gather | solution.py:91
  37.8 18.8 %collective-permute-start = (f32[4]{0:T(128)}, f32[4]{0:T(128)}, u32[]{:S(2)}, u32[]{:S(2)}) collective-permute-start(f32[4]{0:T(128)} %exp.49), channel_id=1, source_target_pairs={{14,0},{0,2},{2,4},{4,6},{6,8},{8,10},{10,12},{12,14},{15,1},{1,3}... | collective-permute-start | bytes 56 | tf_op jit(solution)/shard_map/ppermute | solution.py:17
  45.2 28.8 %collective-permute-start.3 = (f32[4,128,64]{1,2,0:T(8,128)}, f32[4,128,64]{1,2,0:T(8,128)S(1)}, u32[]{:S(2)}, u32[]{:S(2)}) collective-permute-start(f32[4,128,64]{1,2,0:T(8,128)} %fusion.35), channel_id=1, source_target_pairs={{14,0},{0,2},{2,4},{4,6},{6,8},{8,10},{10,12},{12,14},{15,1},{1,3}... | collective-permute-start | bytes 393224 | tf_op jit(solution)/shard_map/ppermute | solution.py:17
  48.5 140.6 %reduce-scatter.2.cloned.1.call-start = ((), (), s32[]{:S(2)}) async-start(), calls=%async_computation.3 | async-start | bytes 3145728 | tf_op jit(solution)/shard_map/reduce_scatter | solution.py:202
  49.5 8.8 %collective-permute-start.8 = (f32[4]{0:T(128)}, f32[4]{0:T(128)}, u32[]{:S(2)}, u32[]{:S(2)}) collective-permute-start(f32[4]{0:T(128)} %exp.54), channel_id=1, source_target_pairs={{2,0},{4,2},{6,4},{8,6},{10,8},{12,10},{14,12},{0,14},{3,1},{5,3},... | collective-permute-start | bytes 56 | tf_op jit(solution)/shard_map/ppermute | solution.py:17
  53.8 19.7 %collective-permute-start.11 = (f32[4,128,64]{1,2,0:T(8,128)}, f32[4,128,64]{1,2,0:T(8,128)S(1)}, u32[]{:S(2)}, u32[]{:S(2)}) collective-permute-start(f32[4,128,64]{1,2,0:T(8,128)} %fusion.33), channel_id=1, source_target_pairs={{2,0},{4,2},{6,4},{8,6},{10,8},{12,10},{14,12},{0,14},{3,1},{5,3},... | collective-permute-start | bytes 393224 | tf_op jit(solution)/shard_map/ppermute | solution.py:17
  56.6 6.5 %collective-permute-start.1 = (f32[4]{0:T(128)}, f32[4]{0:T(128)S(1)}, u32[]{:S(2)}, u32[]{:S(2)}) collective-permute-start(f32[4]{0:T(128)} %collective-permute-done), channel_id=1, source_target_pairs={{14,0},{0,2},{2,4},{4,6},{6,8},{8,10},{10,12},{12,14},{15,1},{1,3}... | collective-permute-start | bytes 56 | tf_op jit(solution)/shard_map/ppermute | solution.py:17
  58.4 5.4 %collective-permute-start.9 = (f32[4]{0:T(128)}, f32[4]{0:T(128)S(1)}, u32[]{:S(2)}, u32[]{:S(2)}) collective-permute-start(f32[4]{0:T(128)} %collective-permute-done.8), channel_id=1, source_target_pairs={{2,0},{4,2},{6,4},{8,6},{10,8},{12,10},{14,12},{0,14},{3,1},{5,3},... | collective-permute-start | bytes 56 | tf_op jit(solution)/shard_map/ppermute | solution.py:17
  63.8 5.4 %collective-permute-start.2 = (f32[4]{0:T(128)S(1)}, f32[4]{0:T(128)S(1)}, u32[]{:S(2)}, u32[]{:S(2)}) collective-permute-start(f32[4]{0:T(128)S(1)} %mul.277), channel_id=1, source_target_pairs={{12,0},{14,2},{0,4},{2,6},{4,8},{6,10},{8,12},{10,14},{13,1},{15,3... | collective-permute-start | bytes 56 | tf_op jit(solution)/shard_map/ppermute | solution.py:17
  64.4 5.1 %collective-permute-start.10 = (f32[4]{0:T(128)S(1)}, f32[4]{0:T(128)S(1)}, u32[]{:S(2)}, u32[]{:S(2)}) collective-permute-start(f32[4]{0:T(128)S(1)} %mul.298), channel_id=1, source_target_pairs={{4,0},{6,2},{8,4},{10,6},{12,8},{14,10},{0,12},{2,14},{5,1},{7,3},... | collective-permute-start | bytes 56 | tf_op jit(solution)/shard_map/ppermute | solution.py:17
  69.1 4.5 %collective-permute-start.7 = (f32[4]{0:T(128)S(1)}, f32[4]{0:T(128)S(1)}, u32[]{:S(2)}, u32[]{:S(2)}) collective-permute-start(f32[4]{0:T(128)S(1)} %mul.278), channel_id=1, source_target_pairs={{8,0},{10,2},{12,4},{14,6},{0,8},{2,10},{4,12},{6,14},{9,1},{11,3}... | collective-permute-start | bytes 56 | tf_op jit(solution)/shard_map/ppermute | solution.py:17
  69.5 4.4 %collective-permute-start.15 = (f32[4]{0:T(128)S(1)}, f32[4]{0:T(128)S(1)}, u32[]{:S(2)}, u32[]{:S(2)}) collective-permute-start(f32[4]{0:T(128)S(1)} %mul.299), channel_id=1, source_target_pairs={{8,0},{10,2},{12,4},{14,6},{0,8},{2,10},{4,12},{6,14},{9,1},{11,3}... | collective-permute-start | bytes 56 | tf_op jit(solution)/shard_map/ppermute | solution.py:17
  73.6 5.9 %collective-permute-start.12 = (f32[4,128,64]{1,2,0:T(8,128)S(1)}, f32[4,128,64]{1,2,0:T(8,128)S(1)}, u32[]{:S(2)}, u32[]{:S(2)}) collective-permute-start(f32[4,128,64]{1,2,0:T(8,128)S(1)} %collective-permute-done.11), channel_id=1, source_target_pairs={{2,0},{4,2},{6,4},{8,6},{10,8},{12,10},{14,12},{0,14},{3,1},{5,3},... | collective-permute-start | bytes 393224 | tf_op jit(solution)/shard_map/ppermute | solution.py:17
  74.0 11.4 %collective-permute-start.4 = (f32[4,128,64]{1,2,0:T(8,128)S(1)}, f32[4,128,64]{1,2,0:T(8,128)S(1)}, u32[]{:S(2)}, u32[]{:S(2)}) collective-permute-start(f32[4,128,64]{1,2,0:T(8,128)S(1)} %collective-permute-done.3), channel_id=1, source_target_pairs={{14,0},{0,2},{2,4},{4,6},{6,8},{8,10},{10,12},{12,14},{15,1},{1,3}... | collective-permute-start | bytes 393224 | tf_op jit(solution)/shard_map/ppermute | solution.py:17
  80.2 6.4 %collective-permute-start.13 = (f32[4,128,64]{1,2,0:T(8,128)S(1)}, f32[4,128,64]{1,2,0:T(8,128)S(1)}, u32[]{:S(2)}, u32[]{:S(2)}) collective-permute-start(f32[4,128,64]{1,2,0:T(8,128)S(1)} %multiply_add_fusion.1), channel_id=1, source_target_pairs={{4,0},{6,2},{8,4},{10,6},{12,8},{14,10},{0,12},{2,14},{5,1},{7,3},... | collective-permute-start | bytes 393224 | tf_op jit(solution)/shard_map/ppermute | solution.py:17
  86.2 11.8 %collective-permute-start.5 = (f32[4,128,64]{1,2,0:T(8,128)S(1)}, f32[4,128,64]{1,2,0:T(8,128)S(1)}, u32[]{:S(2)}, u32[]{:S(2)}) collective-permute-start(f32[4,128,64]{1,2,0:T(8,128)S(1)} %multiply_add_fusion.3), channel_id=1, source_target_pairs={{12,0},{14,2},{0,4},{2,6},{4,8},{6,10},{8,12},{10,14},{13,1},{15,3... | collective-permute-start | bytes 393224 | tf_op jit(solution)/shard_map/ppermute | solution.py:17
  86.7 14.8 %collective-permute-start.14 = (f32[4,128,64]{1,2,0:T(8,128)S(1)}, f32[4,128,64]{1,2,0:T(8,128)S(1)}, u32[]{:S(2)}, u32[]{:S(2)}) collective-permute-start(f32[4,128,64]{1,2,0:T(8,128)S(1)} %multiply_add_fusion), channel_id=1, source_target_pairs={{8,0},{10,2},{12,4},{14,6},{0,8},{2,10},{4,12},{6,14},{9,1},{11,3}... | collective-permute-start | bytes 393224 | tf_op jit(solution)/shard_map/ppermute | solution.py:17
  98.0 10.2 %collective-permute-start.6 = (f32[4,128,64]{1,2,0:T(8,128)S(1)}, f32[4,128,64]{1,2,0:T(8,128)S(1)}, u32[]{:S(2)}, u32[]{:S(2)}) collective-permute-start(f32[4,128,64]{1,2,0:T(8,128)S(1)} %multiply_add_fusion.2), channel_id=1, source_target_pairs={{8,0},{10,2},{12,4},{14,6},{0,8},{2,10},{4,12},{6,14},{9,1},{11,3}... | collective-permute-start | bytes 393224 | tf_op jit(solution)/shard_map/ppermute | solution.py:17
  150.1 28.6 %copy-start.7 = (f32[512]{0:T(512)S(1)}, f32[512]{0:T(512)}, u32[]{:S(2)}) copy-start(f32[512]{0:T(512)} %param.26) | copy-start | bytes 6148
  150.1 28.6 %copy-start.8 = (f32[512]{0:T(512)S(1)}, f32[512]{0:T(512)}, u32[]{:S(2)}) copy-start(f32[512]{0:T(512)} %param.25) | copy-start | bytes 6148
  (12 other events, 65.7 us)
Sparse Core Ops, SparseCore 0:
  8.9 11.7 all-gather.4
  29.6 61.0 all-gather.6
  92.7 49.5 all-gather.8
  181.2 7.7 reduce-scatter.1
where the time goes:
time: 199 us; the launch traced here: 198 us
  waiting for transfers between devices  61.6 us (31%)
  matrix products  41.7 us (21%)
  local copies, waits for them, and re-layouts  33.6 us (17%)
  starting transfers between devices  31 us (16%)
  other arithmetic  15.6 us (8%)
  between operations  14.1 us (7%)
    ppermute x16, starting transfers between devices, passed_along(): return lax.ppermute(block, axis, route)  30.9 us
    all_gather x1, waiting for transfers between devices, local(): value_piece = lax.all_gather(valueset, 'seq', axis=0, tiled=True)  24.4 us
    ppermute x16, waiting for transfers between devices, passed_along(): return lax.ppermute(block, axis, route)  24 us
    unnamed x38, local copies, waits for them, and re-layouts  18 us
    dot_general x4, matrix products, key_block(): jnp.einsum('epq,fpq->pef', query_tile_rows, key_fragment, preferred_eleme...  11.6 us
    dot_general x4, matrix products, key_block(): jnp.einsum('gfa,agn->fgn', weights.astype(jnp.bfloat16), value_piece, pre...  9.27 us
    reduce_scatter x1, waiting for transfers between devices, local(): lax.psum_scatter(partial_out, 'chan', scatter_dimension=1, tiled=True)  7.92 us
    lt x4, other arithmetic, key_block(): key_position < valid_limit  5.19 us
  transfers between devices with their start and end apart: 20, of which 13 were waited for; matrix products, arithmetic and copies ran while one was open for 21% of the time, Pallas kernels for 0%

commit v1 on v0

--- a/solution.py
+++ b/solution.py
@@ -87,8 +87,11 @@
     empty_numer = jnp.zeros((row_count, head_count, HEAD_DIM), jnp.float32)
     empty_total = jnp.zeros((row_count, head_count), jnp.float32)
     carry_pair = (empty_numer, empty_total)
-    key_fragment = lax.all_gather(keyset, "seq", axis=0, tiled=True)
-    value_piece = lax.all_gather(valueset, "seq", axis=0, tiled=True)
+    key_fragment, value_piece = jnp.split(
+        lax.all_gather(jnp.concatenate([keyset, valueset], axis=1), "seq", axis=0, tiled=True),
+        [keyset.shape[1]],
+        axis=1,
+    )
     piece_rows = key_fragment.shape[0]
     block_count = piece_rows // 512
 

time: 199 us -> 193 us (0.970)
  starting transfers between devices: 31 us -> 45.7 us
  waiting for transfers between devices: 61.6 us -> 48.8 us
  local copies, waits for them, and re-layouts: 33.6 us -> 29.7 us
  other arithmetic: 15.6 us -> 12 us
    all_gather x2 -> x1, waiting for transfers between devices: 24.4 us -> 4.54 us  [local(): lax.all_gather(jnp.concatenate([keyset, valueset], axis=1), 'seq', axis=0...]
    ppermute x16, starting transfers between devices: 30.9 us -> 45.6 us  [passed_along(): return lax.ppermute(block, axis, route)]
    split x0 -> x1, local copies, waits for them, and re-layouts: none -> 4.8 us  [local(): jnp.split(lax.all_gather(jnp.concatenate([keyset, valueset], axis=1), 'se...]
    unnamed x38 -> x29, local copies, waits for them, and re-layouts: 18 us -> 13.6 us
    reduce_scatter x1, waiting for transfers between devices: 7.92 us -> 11.7 us  [local(): lax.psum_scatter(partial_out, 'chan', scatter_dimension=1, tiled=True)]
    ppermute x16, waiting for transfers between devices: 24 us -> 27.3 us  [passed_along(): return lax.ppermute(block, axis, route)]
  transfers between devices with their start and end apart: 20 -> 19, of which waited for: 13 -> 10; matrix products, arithmetic and copies ran while one was open for 21% -> 13% of each run, Pallas kernels for 0% -> 0%
where the time goes in v1:
time: 193 us; the launch traced here: 192 us
  waiting for transfers between devices  48.8 us (25%)
  starting transfers between devices  45.7 us (24%)
  matrix products  41.4 us (21%)
  local copies, waits for them, and re-layouts  29.7 us (15%)
  between operations  14.1 us (7%)
  other arithmetic  12 us (6%)
    ppermute x16, starting transfers between devices, passed_along(): return lax.ppermute(block, axis, route)  45.6 us
    ppermute x16, waiting for transfers between devices, passed_along(): return lax.ppermute(block, axis, route)  27.3 us
    unnamed x29, local copies, waits for them, and re-layouts  13.6 us
    reduce_scatter x1, waiting for transfers between devices, local(): lax.psum_scatter(partial_out, 'chan', scatter_dimension=1, tiled=True)  11.7 us
    dot_general x4, matrix products, key_block(): jnp.einsum('epq,fpq->pef', query_tile_rows, key_fragment, preferred_eleme...  11.5 us
    dot_general x4, matrix products, key_block(): jnp.einsum('gfa,agn->fgn', weights.astype(jnp.bfloat16), value_piece, pre...  9.27 us
    lt x4, other arithmetic, key_block(): key_position < valid_limit  5.19 us
    dot_general x1, matrix products, local(): jnp.dot(hidden, attention_in.reshape(model_width, 3 * head_count * HEAD_D...  5.05 us
  transfers between devices with their start and end apart: 19, of which 10 were waited for; matrix products, arithmetic and copies ran while one was open for 13% of the time, Pallas kernels for 0%

profile of v1, /device:TPU:0, one launch (start us, length us, event | category | flops | bytes accessed | tf_op | source)
XLA Modules:
  0.0 191.9 jit_solution(12137568026409129019)
XLA Ops:
  7.3 8.8 %copy.26 = bf16[2048,3,512]{0,2,1:T(8,128)(2,1)} copy(bf16[2048,3,512]{2,0,1:T(8,128)(2,1)} %param.19) | data formatting | bytes 12582912 | tf_op args[4]
  16.2 4.5 %all-gather.3.cloned.1.call-done = bf16[256,2048]{1,0:T(8,128)(2,1)} async-done(((bf16[256,1024]{1,0:T(8,128)(2,1)}), bf16[256,2048]{1,0:T(8,128)(2,1)}) %all-gather.3.cloned.1.call-update) | async-done | bytes 1048592 | tf_op jit(solution)/shard_map/all_gather | solution.py:71
  22.4 5.0 %fusion.17 = f32[256,3,4,128]{0,3,2,1:T(8,128)S(1)} fusion(bf16[3,4,128,2048]{3,2,1,0:T(8,128)(2,1)} %bitcast.162, bf16[256,2048]{1,0:T(8,128)(2,1)S(1)} %fusion.13), kind=kOutput, calls=%fused_computation.30 | convolution fusion | flops 1610612736 | bytes 8912896 | tf_op jit(solution)/shard_map/dot_general | solution.py:79
  36.9 2.9 %fusion.44 = bf16[32,4,8,128]{3,2,1,0:T(8,128)(2,1)S(1)} fusion(bf16[256,2048]{1,0:T(8,128)(2,1)} %copy-done.2, bf16[2048,512]{1,0:T(8,128)(2,1)} %param.20), kind=kOutput, calls=%fused_computation.75 | convolution fusion | flops 537526272 | bytes 3407872 | tf_op jit(solution)/shard_map/dot_general | solution.py:123
  44.5 3.3 %collective-permute-start.8 = (f32[4]{0:T(128)S(1)}, f32[4]{0:T(128)S(1)}, u32[]{:S(2)}, u32[]{:S(2)}) collective-permute-start(f32[4]{0:T(128)S(1)} %exp.54), channel_id=1, source_target_pairs={{2,0},{4,2},{6,4},{8,6},{10,8},{12,10},{14,12},{0,14},{3,1},{5,3},... | collective-permute-start | bytes 56 | tf_op jit(solution)/shard_map/ppermute | solution.py:17
  53.5 2.8 %collective-permute-start.9 = (f32[4]{0:T(128)S(1)}, f32[4]{0:T(128)S(1)}, u32[]{:S(2)}, u32[]{:S(2)}) collective-permute-start(f32[4]{0:T(128)S(1)} %collective-permute-done.8), channel_id=1, source_target_pairs={{2,0},{4,2},{6,4},{8,6},{10,8},{12,10},{14,12},{0,14},{3,1},{5,3},... | collective-permute-start | bytes 56 | tf_op jit(solution)/shard_map/ppermute | solution.py:17
  57.9 3.8 %collective-permute-start.10 = (f32[4]{0:T(128)S(1)}, f32[4]{0:T(128)S(1)}, u32[]{:S(2)}, u32[]{:S(2)}) collective-permute-start(f32[4]{0:T(128)S(1)} %mul.298), channel_id=1, source_target_pairs={{4,0},{6,2},{8,4},{10,6},{12,8},{14,10},{0,12},{2,14},{5,1},{7,3},... | collective-permute-start | bytes 56 | tf_op jit(solution)/shard_map/ppermute | solution.py:17
  63.3 2.9 %collective-permute-start.15 = (f32[4]{0:T(128)S(1)}, f32[4]{0:T(128)S(1)}, u32[]{:S(2)}, u32[]{:S(2)}) collective-permute-start(f32[4]{0:T(128)S(1)} %mul.299), channel_id=1, source_target_pairs={{8,0},{10,2},{12,4},{14,6},{0,8},{2,10},{4,12},{6,14},{9,1},{11,3}... | collective-permute-start | bytes 56 | tf_op jit(solution)/shard_map/ppermute | solution.py:17
  69.8 3.0 %collective-permute-done.12 = f32[4,128,64]{1,2,0:T(8,128)S(1)} collective-permute-done((f32[4,128,64]{1,2,0:T(8,128)S(1)}, f32[4,128,64]{1,2,0:T(8,128)S(1)}, u32[]{:S(2)}, u32[]{:S(2)}) %collective-permute-start.12) | collective-permute-done | bytes 131104 | tf_op jit(solution)/shard_map/ppermute | solution.py:17
  77.7 5.0 %collective-permute-done.13 = f32[4,128,64]{1,2,0:T(8,128)S(1)} collective-permute-done((f32[4,128,64]{1,2,0:T(8,128)S(1)}, f32[4,128,64]{1,2,0:T(8,128)S(1)}, u32[]{:S(2)}, u32[]{:S(2)}) %collective-permute-start.13) | collective-permute-done | bytes 131104 | tf_op jit(solution)/shard_map/ppermute | solution.py:17
  82.8 8.3 %collective-permute-start.14 = (f32[4,128,64]{1,2,0:T(8,128)S(1)}, f32[4,128,64]{1,2,0:T(8,128)S(1)}, u32[]{:S(2)}, u32[]{:S(2)}) collective-permute-start(f32[4,128,64]{1,2,0:T(8,128)S(1)} %multiply_add_fusion), channel_id=1, source_target_pairs={{8,0},{10,2},{12,4},{14,6},{0,8},{2,10},{4,12},{6,14},{9,1},{11,3}... | collective-permute-start | bytes 393224 | tf_op jit(solution)/shard_map/ppermute | solution.py:17
  91.2 14.6 %collective-permute-start.6 = (f32[4,128,64]{1,2,0:T(8,128)S(1)}, f32[4,128,64]{1,2,0:T(8,128)S(1)}, u32[]{:S(2)}, u32[]{:S(2)}) collective-permute-start(f32[4,128,64]{1,2,0:T(8,128)S(1)} %multiply_add_fusion.2), channel_id=1, source_target_pairs={{8,0},{10,2},{12,4},{14,6},{0,8},{2,10},{4,12},{6,14},{9,1},{11,3}... | collective-permute-start | bytes 393224 | tf_op jit(solution)/shard_map/ppermute | solution.py:17
  106.3 12.2 %collective-permute-done.6 = f32[4,128,64]{1,2,0:T(8,128)S(1)} collective-permute-done((f32[4,128,64]{1,2,0:T(8,128)S(1)}, f32[4,128,64]{1,2,0:T(8,128)S(1)}, u32[]{:S(2)}, u32[]{:S(2)}) %collective-permute-start.6) | collective-permute-done | bytes 131104 | tf_op jit(solution)/shard_map/ppermute | solution.py:17
  119.1 4.5 %all-gather.5.cloned.1.call-done = bf16[2048,8,128]{0,2,1:T(8,128)(2,1)} async-done(((bf16[256,8,128]{0,2,1:T(8,128)(2,1)}), bf16[2048,8,128]{0,2,1:T(8,128)(2,1)}) %all-gather.5.cloned.1.call-update) | async-done | bytes 4194320 | tf_op jit(solution)/shard_map/all_gather | solution.py:91
  123.7 4.8 %fusion.78 = (bf16[2048,4,128]{0,2,1:T(8,128)(2,1)}, bf16[2048,4,128]{0,2,1:T(8,128)(2,1)}) fusion(bf16[2048,8,128]{0,2,1:T(8,128)(2,1)} %all-gather.5.cloned.1.call-done), kind=kLoop, calls=%fused_computation.140 | loop fusion | bytes 8388608 | tf_op jit(solution)/shard_map/split | solution.py:90
  128.5 4.5 %reshape.152 = bf16[4,512,4,128]{1,0,3,2:T(4,128)(2,1)} reshape(bf16[2048,4,128]{0,2,1:T(8,128)(2,1)} %get-tuple-element.113) | data formatting | bytes 4194304 | tf_op jit(solution)/shard_map/reshape | solution.py:115
  133.0 4.5 %copy.28 = bf16[4,512,4,128]{3,1,2,0:T(8,128)(2,1)} copy(bf16[4,512,4,128]{1,0,3,2:T(4,128)(2,1)} %reshape.152) | data formatting | bytes 4194304
  137.4 3.1 %copy.68 = bf16[4,16,4,8,512]{4,3,1,0,2:T(8,128)(2,1)} copy(bf16[4,16,4,8,512]{4,3,2,1,0:T(8,128)(2,1)} %bitcast.161) | data formatting | bytes 4194304 | tf_op jit(solution)/shard_map/reshape | solution.py:116
  140.6 28.4 %while.13 = (s32[]{:T(128)}, f32[256,4,128]{0,2,1:T(8,128)S(1)}, f32[256,4]{0,1:T(4,128)S(1)}, bf16[4,512,4,128]{1,3,2,0:T(8,128)(2,1)}, s32[4]{0:T(128)S(1)}, /...) while((s32[]{:T(128)}, f32[256,4,128]{0,2,1:T(8,128)S(1)}, ...), condition=%wide.region_4.5_spmd.clone, body=%wide.region_2.4_spmd.clone.sunk | while | flops 271845376 | bytes 6572676 | solution.py:111
  142.5 2.9 %bitcast_reduce_fusion.2 = (f32[4,256]{1,0:T(4,128)S(1)}, f32[4,512,256]{2,1,0:T(8,128)}) fusion(pred[512]{0:T(512)(128)(4,1)S(1)} %add_compare_fusion.2, bf16[256,4,128]{2,0,1:T(8,128)(2,1)S(1)} %get-tuple-element.211, bf16[4,512,4,128]{3,1,2,0:T(8,128)(2,1)} %get-tuple-element.210, s32[]{:T(128)} %get-tuple-element.194), kind=kOutput, calls=%fused_computation.clone.1 | convolution fusion | flops 135789568 | bytes 2888704 | tf_op jit(solution)/shard_map/while/body/eval_jaxpr/epq,fpq->pef/dot_general | solution.py:33
  149.6 2.9 %bitcast_reduce_fusion.2 = (f32[4,256]{1,0:T(4,128)S(1)}, f32[4,512,256]{2,1,0:T(8,128)}) fusion(pred[512]{0:T(512)(128)(4,1)S(1)} %add_compare_fusion.2, bf16[256,4,128]{2,0,1:T(8,128)(2,1)S(1)} %get-tuple-element.211, bf16[4,512,4,128]{3,1,2,0:T(8,128)(2,1)} %get-tuple-element.210, s32[]{:T(128)} %get-tuple-element.194), kind=kOutput, calls=%fused_computation.clone.1 | convolution fusion | flops 135789568 | bytes 2888704 | tf_op jit(solution)/shard_map/while/body/eval_jaxpr/epq,fpq->pef/dot_general | solution.py:33
  156.7 2.9 %bitcast_reduce_fusion.2 = (f32[4,256]{1,0:T(4,128)S(1)}, f32[4,512,256]{2,1,0:T(8,128)}) fusion(pred[512]{0:T(512)(128)(4,1)S(1)} %add_compare_fusion.2, bf16[256,4,128]{2,0,1:T(8,128)(2,1)S(1)} %get-tuple-element.211, bf16[4,512,4,128]{3,1,2,0:T(8,128)(2,1)} %get-tuple-element.210, s32[]{:T(128)} %get-tuple-element.194), kind=kOutput, calls=%fused_computation.clone.1 | convolution fusion | flops 135789568 | bytes 2888704 | tf_op jit(solution)/shard_map/while/body/eval_jaxpr/epq,fpq->pef/dot_general | solution.py:33
  163.8 2.9 %bitcast_reduce_fusion.2 = (f32[4,256]{1,0:T(4,128)S(1)}, f32[4,512,256]{2,1,0:T(8,128)}) fusion(pred[512]{0:T(512)(128)(4,1)S(1)} %add_compare_fusion.2, bf16[256,4,128]{2,0,1:T(8,128)(2,1)S(1)} %get-tuple-element.211, bf16[4,512,4,128]{3,1,2,0:T(8,128)(2,1)} %get-tuple-element.210, s32[]{:T(128)} %get-tuple-element.194), kind=kOutput, calls=%fused_computation.clone.1 | convolution fusion | flops 135789568 | bytes 2888704 | tf_op jit(solution)/shard_map/while/body/eval_jaxpr/epq,fpq->pef/dot_general | solution.py:33
  171.5 11.7 %reduce-scatter.2.cloned.1.call-done = f32[256,1024]{1,0:T(8,128)} async-done(((f32[256,2048]{1,0:T(8,128)}), f32[256,1024]{1,0:T(8,128)}) %reduce-scatter.2.cloned.1.call-update) | async-done | bytes 1048592 | tf_op jit(solution)/shard_map/reduce_scatter | solution.py:205
  (135 shorter events, 55.6 us)
Async XLA Ops:
  6.5 162.8 %copy-start = (bf16[512,2048]{1,0:T(8,128)(2,1)S(1)}, bf16[512,2048]{1,0:T(8,128)(2,1)}, u32[]{:S(2)}) copy-start(bf16[512,2048]{1,0:T(8,128)(2,1)} %param.27) | copy-start | bytes 6291460
  6.5 14.1 %all-gather.3.cloned.1.call-start = ((), (), s32[]{:S(2)}) async-start(), calls=%async_computation.1 | async-start | bytes 1572864 | tf_op jit(solution)/shard_map/all_gather | solution.py:71
  7.3 13.4 %copy-start.3 = (bf16[16,2048]{1,0:T(8,128)(2,1)S(1)}, bf16[16,2048]{1,0:T(8,128)(2,1)}, u32[]{:S(2)}) copy-start(bf16[16,2048]{1,0:T(8,128)(2,1)} %param.18) | copy-start | bytes 196612
  7.3 13.4 %copy-start.4 = (s32[256]{0:T(256)S(1)}, s32[256]{0:T(256)}, u32[]{:S(2)}) copy-start(s32[256]{0:T(256)} %param.16) | copy-start | bytes 3076
  7.3 116.4 %all-gather.5.cloned.1.call-start = ((), (), s32[]{:S(2)}) async-start(), calls=%async_computation.2 | async-start | bytes 4718592 | tf_op jit(solution)/shard_map/all_gather | solution.py:91
  28.6 154.5 %reduce-scatter.2.cloned.1.call-start = ((), (), s32[]{:S(2)}) async-start(), calls=%async_computation.3 | async-start | bytes 3145728 | tf_op jit(solution)/shard_map/reduce_scatter | solution.py:205
  33.1 18.4 %collective-permute-start = (f32[4]{0:T(128)S(1)}, f32[4]{0:T(128)S(1)}, u32[]{:S(2)}, u32[]{:S(2)}) collective-permute-start(f32[4]{0:T(128)S(1)} %exp.49), channel_id=1, source_target_pairs={{14,0},{0,2},{2,4},{4,6},{6,8},{8,10},{10,12},{12,14},{15,1},{1,3}... | collective-permute-start | bytes 56 | tf_op jit(solution)/shard_map/ppermute | solution.py:17
  40.8 27.3 %collective-permute-start.3 = (f32[4,128,64]{1,2,0:T(8,128)}, f32[4,128,64]{1,2,0:T(8,128)S(1)}, u32[]{:S(2)}, u32[]{:S(2)}) collective-permute-start(f32[4,128,64]{1,2,0:T(8,128)} %fusion.36), channel_id=1, source_target_pairs={{14,0},{0,2},{2,4},{4,6},{6,8},{8,10},{10,12},{12,14},{15,1},{1,3}... | collective-permute-start | bytes 393224 | tf_op jit(solution)/shard_map/ppermute | solution.py:17
  44.5 9.0 %collective-permute-start.8 = (f32[4]{0:T(128)S(1)}, f32[4]{0:T(128)S(1)}, u32[]{:S(2)}, u32[]{:S(2)}) collective-permute-start(f32[4]{0:T(128)S(1)} %exp.54), channel_id=1, source_target_pairs={{2,0},{4,2},{6,4},{8,6},{10,8},{12,10},{14,12},{0,14},{3,1},{5,3},... | collective-permute-start | bytes 56 | tf_op jit(solution)/shard_map/ppermute | solution.py:17
  49.1 18.6 %collective-permute-start.11 = (f32[4,128,64]{1,2,0:T(8,128)S(1)}, f32[4,128,64]{1,2,0:T(8,128)S(1)}, u32[]{:S(2)}, u32[]{:S(2)}) collective-permute-start(f32[4,128,64]{1,2,0:T(8,128)S(1)} %fusion.34), channel_id=1, source_target_pairs={{2,0},{4,2},{6,4},{8,6},{10,8},{12,10},{14,12},{0,14},{3,1},{5,3},... | collective-permute-start | bytes 393224 | tf_op jit(solution)/shard_map/ppermute | solution.py:17
  51.5 6.4 %collective-permute-start.1 = (f32[4]{0:T(128)S(1)}, f32[4]{0:T(128)S(1)}, u32[]{:S(2)}, u32[]{:S(2)}) collective-permute-start(f32[4]{0:T(128)S(1)} %collective-permute-done), channel_id=1, source_target_pairs={{14,0},{0,2},{2,4},{4,6},{6,8},{8,10},{10,12},{12,14},{15,1},{1,3}... | collective-permute-start | bytes 56 | tf_op jit(solution)/shard_map/ppermute | solution.py:17
  53.5 4.5 %collective-permute-start.9 = (f32[4]{0:T(128)S(1)}, f32[4]{0:T(128)S(1)}, u32[]{:S(2)}, u32[]{:S(2)}) collective-permute-start(f32[4]{0:T(128)S(1)} %collective-permute-done.8), channel_id=1, source_target_pairs={{2,0},{4,2},{6,4},{8,6},{10,8},{12,10},{14,12},{0,14},{3,1},{5,3},... | collective-permute-start | bytes 56 | tf_op jit(solution)/shard_map/ppermute | solution.py:17
  57.9 5.3 %collective-permute-start.2 = (f32[4]{0:T(128)S(1)}, f32[4]{0:T(128)S(1)}, u32[]{:S(2)}, u32[]{:S(2)}) collective-permute-start(f32[4]{0:T(128)S(1)} %mul.277), channel_id=1, source_target_pairs={{12,0},{14,2},{0,4},{2,6},{4,8},{6,10},{8,12},{10,14},{13,1},{15,3... | collective-permute-start | bytes 56 | tf_op jit(solution)/shard_map/ppermute | solution.py:17
  57.9 5.3 %collective-permute-start.10 = (f32[4]{0:T(128)S(1)}, f32[4]{0:T(128)S(1)}, u32[]{:S(2)}, u32[]{:S(2)}) collective-permute-start(f32[4]{0:T(128)S(1)} %mul.298), channel_id=1, source_target_pairs={{4,0},{6,2},{8,4},{10,6},{12,8},{14,10},{0,12},{2,14},{5,1},{7,3},... | collective-permute-start | bytes 56 | tf_op jit(solution)/shard_map/ppermute | solution.py:17
  63.3 4.4 %collective-permute-start.7 = (f32[4]{0:T(128)S(1)}, f32[4]{0:T(128)S(1)}, u32[]{:S(2)}, u32[]{:S(2)}) collective-permute-start(f32[4]{0:T(128)S(1)} %mul.278), channel_id=1, source_target_pairs={{8,0},{10,2},{12,4},{14,6},{0,8},{2,10},{4,12},{6,14},{9,1},{11,3}... | collective-permute-start | bytes 56 | tf_op jit(solution)/shard_map/ppermute | solution.py:17
  63.3 4.8 %collective-permute-start.15 = (f32[4]{0:T(128)S(1)}, f32[4]{0:T(128)S(1)}, u32[]{:S(2)}, u32[]{:S(2)}) collective-permute-start(f32[4]{0:T(128)S(1)} %mul.299), channel_id=1, source_target_pairs={{8,0},{10,2},{12,4},{14,6},{0,8},{2,10},{4,12},{6,14},{9,1},{11,3}... | collective-permute-start | bytes 56 | tf_op jit(solution)/shard_map/ppermute | solution.py:17
  67.7 5.1 %collective-permute-start.12 = (f32[4,128,64]{1,2,0:T(8,128)S(1)}, f32[4,128,64]{1,2,0:T(8,128)S(1)}, u32[]{:S(2)}, u32[]{:S(2)}) collective-permute-start(f32[4,128,64]{1,2,0:T(8,128)S(1)} %collective-permute-done.11), channel_id=1, source_target_pairs={{2,0},{4,2},{6,4},{8,6},{10,8},{12,10},{14,12},{0,14},{3,1},{5,3},... | collective-permute-start | bytes 393224 | tf_op jit(solution)/shard_map/ppermute | solution.py:17
  68.1 7.9 %collective-permute-start.4 = (f32[4,128,64]{1,2,0:T(8,128)S(1)}, f32[4,128,64]{1,2,0:T(8,128)S(1)}, u32[]{:S(2)}, u32[]{:S(2)}) collective-permute-start(f32[4,128,64]{1,2,0:T(8,128)S(1)} %collective-permute-done.3), channel_id=1, source_target_pairs={{14,0},{0,2},{2,4},{4,6},{6,8},{8,10},{10,12},{12,14},{15,1},{1,3}... | collective-permute-start | bytes 393224 | tf_op jit(solution)/shard_map/ppermute | solution.py:17
  72.9 9.8 %collective-permute-start.13 = (f32[4,128,64]{1,2,0:T(8,128)S(1)}, f32[4,128,64]{1,2,0:T(8,128)S(1)}, u32[]{:S(2)}, u32[]{:S(2)}) collective-permute-start(f32[4,128,64]{1,2,0:T(8,128)S(1)} %multiply_add_fusion.1), channel_id=1, source_target_pairs={{4,0},{6,2},{8,4},{10,6},{12,8},{14,10},{0,12},{2,14},{5,1},{7,3},... | collective-permute-start | bytes 393224 | tf_op jit(solution)/shard_map/ppermute | solution.py:17
  76.1 15.0 %collective-permute-start.5 = (f32[4,128,64]{1,2,0:T(8,128)S(1)}, f32[4,128,64]{1,2,0:T(8,128)S(1)}, u32[]{:S(2)}, u32[]{:S(2)}) collective-permute-start(f32[4,128,64]{1,2,0:T(8,128)S(1)} %multiply_add_fusion.3), channel_id=1, source_target_pairs={{12,0},{14,2},{0,4},{2,6},{4,8},{6,10},{8,12},{10,14},{13,1},{15,3... | collective-permute-start | bytes 393224 | tf_op jit(solution)/shard_map/ppermute | solution.py:17
  82.8 23.0 %collective-permute-start.14 = (f32[4,128,64]{1,2,0:T(8,128)S(1)}, f32[4,128,64]{1,2,0:T(8,128)S(1)}, u32[]{:S(2)}, u32[]{:S(2)}) collective-permute-start(f32[4,128,64]{1,2,0:T(8,128)S(1)} %multiply_add_fusion), channel_id=1, source_target_pairs={{8,0},{10,2},{12,4},{14,6},{0,8},{2,10},{4,12},{6,14},{9,1},{11,3}... | collective-permute-start | bytes 393224 | tf_op jit(solution)/shard_map/ppermute | solution.py:17
  91.2 27.4 %collective-permute-start.6 = (f32[4,128,64]{1,2,0:T(8,128)S(1)}, f32[4,128,64]{1,2,0:T(8,128)S(1)}, u32[]{:S(2)}, u32[]{:S(2)}) collective-permute-start(f32[4,128,64]{1,2,0:T(8,128)S(1)} %multiply_add_fusion.2), channel_id=1, source_target_pairs={{8,0},{10,2},{12,4},{14,6},{0,8},{2,10},{4,12},{6,14},{9,1},{11,3}... | collective-permute-start | bytes 393224 | tf_op jit(solution)/shard_map/ppermute | solution.py:17
  140.6 28.5 %copy-start.5 = (f32[512]{0:T(512)S(1)}, f32[512]{0:T(512)}, u32[]{:S(2)}) copy-start(f32[512]{0:T(512)} %param.26) | copy-start | bytes 6148
  140.6 28.5 %copy-start.6 = (f32[512]{0:T(512)S(1)}, f32[512]{0:T(512)}, u32[]{:S(2)}) copy-start(f32[512]{0:T(512)} %param.25) | copy-start | bytes 6148
  (7 other events, 32.0 us)
Sparse Core Ops, SparseCore 0:
  8.9 11.7 all-gather.2
  28.7 94.8 all-gather.4
  171.6 11.5 reduce-scatter.1
